TPU v7x, 32 devices: a whole 2x2x4 slice. The times are simulated.
32 devices in a mesh: grp: 2 (over x), view: 16 (over z, y, core).
Axes of the slice: x: 2, y: 2, z: 4, core: 2. Of those that a mesh axis runs over, the one named last changes fastest.
Arguments:
- features: float32 [32, 32, 8, 256], P(('grp', 'view')), parts along dimension 0, may hold values from -96 to 96, as said below
- offsets: int32 [32, 128], P(('grp', 'view')), parts along dimension 0, may hold values from 0 to 31
- conf_bins: int32 [16, 256], P('grp'), parts along dimension 0, may hold values from 0 to 3
- plane_depths: float32 [128], P('view'), may hold values from 1 to 10
Outputs:
- cost_volume: float32 [128, 16, 256], P('view', 'grp'), parts along dimension 1
- depth_map: float32 [16, 256], P('grp'), parts along dimension 0
There are 2 independent parts, one for each index of `grp`. A program takes and returns all parts, laid end to end along the dimension named above; an argument that names none is the same for every part. Nothing has to cross between parts.
Inputs may be any that keep to these rules, and one draw needn't show every extreme that they name: `features`: feature entries may be large on some rows.
All inputs are finite; a program needn't handle non-finite values.
Results may differ from a plain program's by a relative error of at most 0.0003.
Values sent between devices are 32-bit elements; how exact they have to be, the bound alone decides.
A program may use at most 128 MiB of HBM per device.

v0:
```python
import math

import jax
import jax.numpy as jnp
from jax import lax
from jax.sharding import PartitionSpec as P

ITERS = 4


def extended(block, sides, width):
    for axis, dim in sides:
        count = lax.axis_size(axis)
        forward = [(i, i + 1) for i in range(count - 1)]
        backward = [(target, source) for source, target in forward]
        low = lax.ppermute(
            lax.slice_in_dim(block, block.shape[dim] - width, None, axis=dim), axis, forward
        )
        high = lax.ppermute(lax.slice_in_dim(block, 0, width, axis=dim), axis, backward)
        block = jnp.concatenate([low, block, high], axis=dim)
    return block


def joined(value, axis, join):
    pieces = jax.tree.map(lambda part: lax.all_gather(part, axis), value)
    head = jax.tree.map(lambda part: part[0], pieces)
    tail = jax.tree.map(lambda part: part[1:], pieces)
    so_far, _ = lax.scan(lambda so_far, piece: (join(so_far, piece), None), head, tail)
    return so_far


def warp_tile(tile, shift):
    pad = tile.shape[2] // 8
    padded = jnp.pad(tile, ((0, 0), (0, 0), (pad, 0)))
    return lax.dynamic_slice_in_dim(padded, (pad - shift).astype(jnp.int32), tile.shape[2], 2)


def warp_planes(tile, shifts):
    return jax.vmap(lambda shift: warp_tile(tile, shift))(shifts)


def combine_soft(first, second):
    top = jnp.maximum(first[0], second[0])
    scale_a = jnp.exp(first[0] - top)
    scale_b = jnp.exp(second[0] - top)
    return (top, first[1] * scale_a + second[1] * scale_b, first[2] * scale_a + second[2] * scale_b)


def per_device(features, offsets, conf_bins, plane_depths):
    count = lax.axis_size("view")
    owned = plane_depths.shape[0]
    first_plane = lax.axis_index("view") * owned
    blank = jnp.zeros((owned,) + features.shape[1:], jnp.float32)
    tiles = lax.all_gather(features, "view", axis=0, tiled=True)
    shifts = lax.all_gather(offsets, "view", axis=0, tiled=True)
    chosen = lax.dynamic_slice_in_dim(shifts, first_plane, owned, 1)
    number = tiles.shape[0]
    per_block = math.gcd(number, 4)
    tile_blocks = tiles.reshape((number // per_block, per_block) + tiles.shape[1:])
    shift_blocks = chosen.reshape((number // per_block, per_block, owned))

    def visit(inner, item):
        warped = jax.vmap(warp_planes)(item[0], item[1])
        return (
            (inner[0] + jnp.sum(warped, axis=0), inner[1] + jnp.sum(warped * warped, axis=0)),
            None,
        )

    result, unused = lax.scan(visit, (blank, blank), (tile_blocks, shift_blocks))
    total, square = result
    mean = total / count
    cost = jnp.mean(square / count - mean * mean, axis=1)
    conf = (conf_bins.astype(jnp.float32) + 1.0) * 0.25
    for step in range(ITERS):
        rims = extended(cost, (("view", 0),), 1)
        inner = jnp.pad(cost, ((0, 0), (1, 1), (1, 1)))
        beside = rims[2:] + rims[:-2]
        beside = beside + inner[:, 2:, 1:-1] + inner[:, :-2, 1:-1]
        beside = beside + inner[:, 1:-1, 2:] + inner[:, 1:-1, :-2]
        cost = cost + 0.15 * conf * (beside - 6.0 * cost)
    logits = -cost
    local_peak = jnp.max(logits, axis=0)
    weights = jnp.exp(logits - local_peak)
    local_sum = jnp.sum(weights, axis=0)
    local_depth = jnp.sum(weights * plane_depths[:, None, None], axis=0)
    top, denom, numer = joined((local_peak, local_sum, local_depth), "view", combine_soft)
    return (cost, numer / denom)


def solution(mesh):
    in_specs = (
        P(("grp", "view"), None, None, None),
        P(("grp", "view"), None),
        P("grp", None),
        P("view"),
    )
    out_specs = (P("view", "grp", None), P("grp", None))
    return jax.shard_map(
        per_device, mesh=mesh, in_specs=in_specs, out_specs=out_specs, check_vma=False
    )
```

profile of v0, /device:TPU:0, one launch (start us, length us, event | category | flops | bytes accessed | tf_op | source)
XLA Modules:
  0.0 427.1 jit_solution(11088320836404151226)
XLA Ops:
  7.2 0.0 all-gather.6.cloned.1.call-start
  7.2 0.7 all-gather.6.cloned.1.call-update
  7.9 23.4 %all-gather.3 = s32[16,1,128]{2,1,0:T(1,128)S(1)} all-gather(s32[1,1,128]{2,1,0:T(1,128)} %bitcast.55), channel_id=1, replica_groups=mesh['grp'=2,'view'=16] {'view'}, dimensions={0}, use_global_device_ids=true | all-gather | bytes 8704 | tf_op jit(solution)/shard_map/all_gather | solution.py:55
  31.4 0.1 constant_dynamic-slice_fusion.1
  31.4 31.8 %all-gather.6.cloned.1.call-done = f32[16,32,8,256]{3,2,1,0:T(8,128)} async-done(((f32[1,32,8,256]{3,2,1,0:T(8,128)}), f32[16,32,8,256]{3,2,1,0:T(8,128)}) %all-gather.6.cloned.1.call-update) | async-done | bytes 4194320 | tf_op jit(solution)/shard_map/all_gather | solution.py:54
  63.3 258.6 %while.30 = (s32[]{:T(128)}, f32[8,32,8,256]{1,2,3,0:T(8,128)}, f32[8,32,8,256]{1,2,3,0:T(8,128)}, f32[4,4,32,8,256]{4,3,2,1,0:T(8,128)}, s32[4,4,8]{2,1,0:T(4,128)S(1)}, /*index=5*/s32[]{:T(128)}, f32[]{:T(128)}, s32[]{:T(128)}) while((s32[]{:T(128)}, f32[8,32,8,256]{1,2,3,0:T(8,128)}, f32[8,32,8,256]{1,2,3,0:T(8,128)}, ...), condition=%wide.region_3.4_spmd.clone, body=%wide.region_0.3_spmd.clone.sunk | while | flops 7340323 | bytes 48366696 | solution.py:69
  63.3 1.3 constant_dynamic-slice_fusion.3
  64.6 4.5 %copy.117 = f32[1,4,32,8,256]{2,3,1,4,0:T(8,128)} copy(f32[1,4,32,8,256]{4,3,2,1,0:T(8,128)S(1)} %constant_dynamic-slice_fusion.3) | data formatting | bytes 2097152 | tf_op jit(solution)/shard_map/while/body/jit(dynamic_index_in_dim)/dynamic_slice | solution.py:69
  69.1 5.0 %pad.203 = f32[4,32,8,288]{1,2,0,3:T(8,128)} pad(f32[4,32,8,256]{1,2,0,3:T(8,128)} %bitcast.51, f32[]{:T(128)} %constant.62.clone.6..sunk), padding=0_0x0_0x0_0x32_0 | pad | bytes 2228228 | tf_op jit(solution)/shard_map/while/body/eval_jaxpr/vmap(vmap(jit(_pad)))/pad | solution.py:34
  74.1 0.1 reshape.80
  74.2 17.0 %gather_fusion = f32[32,32,8,256]{1,2,3,0:T(8,128)} fusion(f32[4,32,8,288]{1,2,0,3:T(8,128)} %pad.203, s32[32]{0:T(128)S(1)} %reshape.80), kind=kCustom, calls=%fused_computation.clone.clone.1 | custom fusion | bytes 16777728 | tf_op jit(solution)/shard_map/while/body/eval_jaxpr/vmap(vmap())/gather | solution.py:35
  91.2 20.8 %multiply_reduce_fusion.3 = (f32[8,32,8,256]{1,2,3,0:T(8,128)}, f32[8,32,8,256]{1,2,3,0:T(8,128)}) fusion(f32[4,8,32,8,256]{2,3,4,1,0:T(8,128)} %bitcast.50), kind=kLoop, calls=%fused_computation.9.clone.1 | loop fusion | flops 5242880 | bytes 12582912 | tf_op jit(solution)/shard_map/while/body/eval_jaxpr/reduce_sum | solution.py:65
  111.9 11.2 %select_add_fusion.3 = (f32[8,32,8,256]{1,2,3,0:T(8,128)}, f32[8,32,8,256]{1,2,3,0:T(8,128)}) fusion(f32[8,32,8,256]{1,2,3,0:T(8,128)} %get-tuple-element.310, f32[8,32,8,256]{1,2,3,0:T(8,128)} %get-tuple-element.324, pred[]{:T(512)S(6)} %compare.9, f32[8,32,8,256]{1,2,3,0:T(8,128)} %get-tuple-element.311, f32[8,32,8,256]{1,2,3,0:T(8,128)} %get-tuple-element.323), kind=kLoop, calls=%fused_computation.10.clone.1 | loop fusion | flops 2097152 | bytes 12582913 | tf_op jit(solution)/shard_map/while/body/eval_jaxpr/add | solution.py:65
  123.2 1.3 constant_dynamic-slice_fusion.3
  124.5 4.5 %copy.117 = f32[1,4,32,8,256]{2,3,1,4,0:T(8,128)} copy(f32[1,4,32,8,256]{4,3,2,1,0:T(8,128)S(1)} %constant_dynamic-slice_fusion.3) | data formatting | bytes 2097152 | tf_op jit(solution)/shard_map/while/body/jit(dynamic_index_in_dim)/dynamic_slice | solution.py:69
  129.0 5.0 %pad.203 = f32[4,32,8,288]{1,2,0,3:T(8,128)} pad(f32[4,32,8,256]{1,2,0,3:T(8,128)} %bitcast.51, f32[]{:T(128)} %constant.62.clone.6..sunk), padding=0_0x0_0x0_0x32_0 | pad | bytes 2228228 | tf_op jit(solution)/shard_map/while/body/eval_jaxpr/vmap(vmap(jit(_pad)))/pad | solution.py:34
  133.9 0.1 reshape.80
  134.0 17.0 %gather_fusion = f32[32,32,8,256]{1,2,3,0:T(8,128)} fusion(f32[4,32,8,288]{1,2,0,3:T(8,128)} %pad.203, s32[32]{0:T(128)S(1)} %reshape.80), kind=kCustom, calls=%fused_computation.clone.clone.1 | custom fusion | bytes 16777728 | tf_op jit(solution)/shard_map/while/body/eval_jaxpr/vmap(vmap())/gather | solution.py:35
  151.0 20.8 %multiply_reduce_fusion.3 = (f32[8,32,8,256]{1,2,3,0:T(8,128)}, f32[8,32,8,256]{1,2,3,0:T(8,128)}) fusion(f32[4,8,32,8,256]{2,3,4,1,0:T(8,128)} %bitcast.50), kind=kLoop, calls=%fused_computation.9.clone.1 | loop fusion | flops 5242880 | bytes 12582912 | tf_op jit(solution)/shard_map/while/body/eval_jaxpr/reduce_sum | solution.py:65
  171.8 17.6 %select_add_fusion.3 = (f32[8,32,8,256]{1,2,3,0:T(8,128)}, f32[8,32,8,256]{1,2,3,0:T(8,128)}) fusion(f32[8,32,8,256]{1,2,3,0:T(8,128)} %get-tuple-element.310, f32[8,32,8,256]{1,2,3,0:T(8,128)} %get-tuple-element.324, pred[]{:T(512)S(6)} %compare.9, f32[8,32,8,256]{1,2,3,0:T(8,128)} %get-tuple-element.311, f32[8,32,8,256]{1,2,3,0:T(8,128)} %get-tuple-element.323), kind=kLoop, calls=%fused_computation.10.clone.1 | loop fusion | flops 2097152 | bytes 12582913 | tf_op jit(solution)/shard_map/while/body/eval_jaxpr/add | solution.py:65
  189.4 1.3 constant_dynamic-slice_fusion.3
  190.7 4.5 %copy.117 = f32[1,4,32,8,256]{2,3,1,4,0:T(8,128)} copy(f32[1,4,32,8,256]{4,3,2,1,0:T(8,128)S(1)} %constant_dynamic-slice_fusion.3) | data formatting | bytes 2097152 | tf_op jit(solution)/shard_map/while/body/jit(dynamic_index_in_dim)/dynamic_slice | solution.py:69
  195.2 5.0 %pad.203 = f32[4,32,8,288]{1,2,0,3:T(8,128)} pad(f32[4,32,8,256]{1,2,0,3:T(8,128)} %bitcast.51, f32[]{:T(128)} %constant.62.clone.6..sunk), padding=0_0x0_0x0_0x32_0 | pad | bytes 2228228 | tf_op jit(solution)/shard_map/while/body/eval_jaxpr/vmap(vmap(jit(_pad)))/pad | solution.py:34
  200.2 0.1 reshape.80
  200.3 17.0 %gather_fusion = f32[32,32,8,256]{1,2,3,0:T(8,128)} fusion(f32[4,32,8,288]{1,2,0,3:T(8,128)} %pad.203, s32[32]{0:T(128)S(1)} %reshape.80), kind=kCustom, calls=%fused_computation.clone.clone.1 | custom fusion | bytes 16777728 | tf_op jit(solution)/shard_map/while/body/eval_jaxpr/vmap(vmap())/gather | solution.py:35
  217.3 20.8 %multiply_reduce_fusion.3 = (f32[8,32,8,256]{1,2,3,0:T(8,128)}, f32[8,32,8,256]{1,2,3,0:T(8,128)}) fusion(f32[4,8,32,8,256]{2,3,4,1,0:T(8,128)} %bitcast.50), kind=kLoop, calls=%fused_computation.9.clone.1 | loop fusion | flops 5242880 | bytes 12582912 | tf_op jit(solution)/shard_map/while/body/eval_jaxpr/reduce_sum | solution.py:65
  238.0 17.6 %select_add_fusion.3 = (f32[8,32,8,256]{1,2,3,0:T(8,128)}, f32[8,32,8,256]{1,2,3,0:T(8,128)}) fusion(f32[8,32,8,256]{1,2,3,0:T(8,128)} %get-tuple-element.310, f32[8,32,8,256]{1,2,3,0:T(8,128)} %get-tuple-element.324, pred[]{:T(512)S(6)} %compare.9, f32[8,32,8,256]{1,2,3,0:T(8,128)} %get-tuple-element.311, f32[8,32,8,256]{1,2,3,0:T(8,128)} %get-tuple-element.323), kind=kLoop, calls=%fused_computation.10.clone.1 | loop fusion | flops 2097152 | bytes 12582913 | tf_op jit(solution)/shard_map/while/body/eval_jaxpr/add | solution.py:65
  255.6 1.3 constant_dynamic-slice_fusion.3
  256.9 4.5 %copy.117 = f32[1,4,32,8,256]{2,3,1,4,0:T(8,128)} copy(f32[1,4,32,8,256]{4,3,2,1,0:T(8,128)S(1)} %constant_dynamic-slice_fusion.3) | data formatting | bytes 2097152 | tf_op jit(solution)/shard_map/while/body/jit(dynamic_index_in_dim)/dynamic_slice | solution.py:69
  261.4 5.0 %pad.203 = f32[4,32,8,288]{1,2,0,3:T(8,128)} pad(f32[4,32,8,256]{1,2,0,3:T(8,128)} %bitcast.51, f32[]{:T(128)} %constant.62.clone.6..sunk), padding=0_0x0_0x0_0x32_0 | pad | bytes 2228228 | tf_op jit(solution)/shard_map/while/body/eval_jaxpr/vmap(vmap(jit(_pad)))/pad | solution.py:34
  266.4 0.1 reshape.80
  266.5 17.0 %gather_fusion = f32[32,32,8,256]{1,2,3,0:T(8,128)} fusion(f32[4,32,8,288]{1,2,0,3:T(8,128)} %pad.203, s32[32]{0:T(128)S(1)} %reshape.80), kind=kCustom, calls=%fused_computation.clone.clone.1 | custom fusion | bytes 16777728 | tf_op jit(solution)/shard_map/while/body/eval_jaxpr/vmap(vmap())/gather | solution.py:35
  283.5 20.8 %multiply_reduce_fusion.3 = (f32[8,32,8,256]{1,2,3,0:T(8,128)}, f32[8,32,8,256]{1,2,3,0:T(8,128)}) fusion(f32[4,8,32,8,256]{2,3,4,1,0:T(8,128)} %bitcast.50), kind=kLoop, calls=%fused_computation.9.clone.1 | loop fusion | flops 5242880 | bytes 12582912 | tf_op jit(solution)/shard_map/while/body/eval_jaxpr/reduce_sum | solution.py:65
  304.3 17.6 %select_add_fusion.3 = (f32[8,32,8,256]{1,2,3,0:T(8,128)}, f32[8,32,8,256]{1,2,3,0:T(8,128)}) fusion(f32[8,32,8,256]{1,2,3,0:T(8,128)} %get-tuple-element.310, f32[8,32,8,256]{1,2,3,0:T(8,128)} %get-tuple-element.324, pred[]{:T(512)S(6)} %compare.9, f32[8,32,8,256]{1,2,3,0:T(8,128)} %get-tuple-element.311, f32[8,32,8,256]{1,2,3,0:T(8,128)} %get-tuple-element.323), kind=kLoop, calls=%fused_computation.10.clone.1 | loop fusion | flops 2097152 | bytes 12582913 | tf_op jit(solution)/shard_map/while/body/eval_jaxpr/add | solution.py:65
  321.9 8.1 %subtract_reduce_fusion = f32[8,8,256]{1,2,0:T(8,128)S(1)} fusion(f32[8,32,8,256]{1,2,3,0:T(8,128)} %get-tuple-element.108, f32[8,32,8,256]{1,2,3,0:T(8,128)} %get-tuple-element.107), kind=kLoop, calls=%fused_computation.17 | loop fusion | flops 2605056 | bytes 4259840 | tf_op jit(solution)/shard_map/reduce_sum | solution.py:72
  329.9 0.3 copy.103
  330.3 1.3 collective-permute-start
  331.6 3.0 collective-permute-start.1
  334.6 0.0 collective-permute-done
  334.6 0.8 collective-permute-done.1
  335.4 0.1 fusion.12
  335.5 1.3 collective-permute-start.2
  336.8 4.0 collective-permute-start.3
  340.8 0.0 collective-permute-done.2
  340.8 0.8 collective-permute-done.3
  341.6 0.1 fusion.19
  341.8 1.3 collective-permute-start.4
  343.1 4.8 %collective-permute-start.5 = (f32[1,8,256]{2,1,0:T(8,128)S(1)}, f32[1,8,256]{2,1,0:T(8,128)S(1)}, u32[]{:S(2)}, u32[]{:S(2)}) collective-permute-start(f32[1,8,256]{2,1,0:T(8,128)S(1)} %get-tuple-element.223), channel_id=1, source_target_pairs={{0,1},{1,2},{2,3},{3,4},{4,5},{5,6},{6,7},{7,8},{8,9},{9,10},{10,1... | collective-permute-start | bytes 24584 | tf_op jit(solution)/shard_map/ppermute | solution.py:16
  347.8 0.0 collective-permute-done.4
  347.8 0.8 collective-permute-done.5
  348.6 0.1 fusion.26
  348.8 1.3 collective-permute-start.6
  350.1 4.8 %collective-permute-start.7 = (f32[1,8,256]{2,1,0:T(8,128)S(1)}, f32[1,8,256]{2,1,0:T(8,128)S(1)}, u32[]{:S(2)}, u32[]{:S(2)}) collective-permute-start(f32[1,8,256]{2,1,0:T(8,128)S(1)} %get-tuple-element.221), channel_id=1, source_target_pairs={{0,1},{1,2},{2,3},{3,4},{4,5},{5,6},{6,7},{7,8},{8,9},{9,10},{10,1... | collective-permute-start | bytes 24584 | tf_op jit(solution)/shard_map/ppermute | solution.py:16
  354.9 0.0 collective-permute-done.6
  354.9 0.8 collective-permute-done.7
  355.7 0.1 negate_reduce_fusion
  355.8 0.0 copy-start
  355.8 0.0 copy-done.2
  355.8 0.1 multiply_reduce_fusion.1
  355.9 25.6 %all-gather.1 = f32[128,256]{1,0:T(8,128)S(1)} all-gather(f32[8,256]{1,0:T(8,128)S(1)} %get-tuple-element.189), channel_id=3, replica_groups=mesh['grp'=2,'view'=16] {'view'}, dimensions={0}, use_global_device_ids=true | all-gather | bytes 139264 | tf_op jit(solution)/shard_map/all_gather | solution.py:25
  381.5 17.8 %all-gather.2 = f32[128,256]{1,0:T(8,128)S(1)} all-gather(f32[8,256]{1,0:T(8,128)S(1)} %get-tuple-element.188), channel_id=4, replica_groups=mesh['grp'=2,'view'=16] {'view'}, dimensions={0}, use_global_device_ids=true | all-gather | bytes 139264 | tf_op jit(solution)/shard_map/all_gather | solution.py:25
  399.3 19.1 %all-gather = f32[128,256]{1,0:T(8,128)S(1)} all-gather(f32[8,256]{1,0:T(8,128)S(1)} %get-tuple-element.216), channel_id=2, replica_groups=mesh['grp'=2,'view'=16] {'view'}, dimensions={0}, use_global_device_ids=true | all-gather | bytes 139264 | tf_op jit(solution)/shard_map/all_gather | solution.py:25
  418.5 1.2 while.29
  419.6 0.6 div.19
  (67 shorter events, 0.8 us)
Async XLA Ops:
  7.2 56.1 %all-gather.6.cloned.1.call-start = ((), (), s32[]{:S(2)}) async-start(), calls=%async_computation | async-start | bytes 4456448 | tf_op jit(solution)/shard_map/all_gather | solution.py:54
  321.9 12.7 %copy-start.1 = (s32[8,256]{1,0:T(8,128)S(1)}, s32[8,256]{1,0:T(8,128)}, u32[]{:S(2)}) copy-start(s32[8,256]{1,0:T(8,128)} %param.10) | copy-start | bytes 24580
  321.9 33.9 %copy-start.2 = (f32[8]{0:T(128)S(1)}, f32[8]{0:T(128)}, u32[]{:S(2)}) copy-start(f32[8]{0:T(128)} %param.11) | copy-start | bytes 100
  330.3 4.4 %collective-permute-start = (f32[1,8,256]{2,1,0:T(8,128)S(1)}, f32[1,8,256]{2,1,0:T(8,128)S(1)}, u32[]{:S(2)}, u32[]{:S(2)}) collective-permute-start(f32[1,8,256]{2,1,0:T(8,128)S(1)} %get-tuple-element.226), channel_id=1, source_target_pairs={{1,0},{2,1},{3,2},{4,3},{5,4},{6,5},{7,6},{8,7},{9,8},{10,9},{11,1... | collective-permute-start | bytes 24584 | tf_op jit(solution)/shard_map/ppermute | solution.py:19
  331.6 3.8 collective-permute-start.1
  335.5 5.3 %collective-permute-start.2 = (f32[1,8,256]{2,1,0:T(8,128)S(1)}, f32[1,8,256]{2,1,0:T(8,128)S(1)}, u32[]{:S(2)}, u32[]{:S(2)}) collective-permute-start(f32[1,8,256]{2,1,0:T(8,128)S(1)} %get-tuple-element.224), channel_id=1, source_target_pairs={{1,0},{2,1},{3,2},{4,3},{5,4},{6,5},{7,6},{8,7},{9,8},{10,9},{11,1... | collective-permute-start | bytes 24584 | tf_op jit(solution)/shard_map/ppermute | solution.py:19
  336.8 4.8 %collective-permute-start.3 = (f32[1,8,256]{2,1,0:T(8,128)S(1)}, f32[1,8,256]{2,1,0:T(8,128)S(1)}, u32[]{:S(2)}, u32[]{:S(2)}) collective-permute-start(f32[1,8,256]{2,1,0:T(8,128)S(1)} %get-tuple-element.225), channel_id=1, source_target_pairs={{0,1},{1,2},{2,3},{3,4},{4,5},{5,6},{6,7},{7,8},{8,9},{9,10},{10,1... | collective-permute-start | bytes 24584 | tf_op jit(solution)/shard_map/ppermute | solution.py:16
  341.8 6.1 %collective-permute-start.4 = (f32[1,8,256]{2,1,0:T(8,128)S(1)}, f32[1,8,256]{2,1,0:T(8,128)S(1)}, u32[]{:S(2)}, u32[]{:S(2)}) collective-permute-start(f32[1,8,256]{2,1,0:T(8,128)S(1)} %get-tuple-element.222), channel_id=1, source_target_pairs={{1,0},{2,1},{3,2},{4,3},{5,4},{6,5},{7,6},{8,7},{9,8},{10,9},{11,1... | collective-permute-start | bytes 24584 | tf_op jit(solution)/shard_map/ppermute | solution.py:19
  343.1 5.6 %collective-permute-start.5 = (f32[1,8,256]{2,1,0:T(8,128)S(1)}, f32[1,8,256]{2,1,0:T(8,128)S(1)}, u32[]{:S(2)}, u32[]{:S(2)}) collective-permute-start(f32[1,8,256]{2,1,0:T(8,128)S(1)} %get-tuple-element.223), channel_id=1, source_target_pairs={{0,1},{1,2},{2,3},{3,4},{4,5},{5,6},{6,7},{7,8},{8,9},{9,10},{10,1... | collective-permute-start | bytes 24584 | tf_op jit(solution)/shard_map/ppermute | solution.py:16
  348.8 6.1 %collective-permute-start.6 = (f32[1,8,256]{2,1,0:T(8,128)S(1)}, f32[1,8,256]{2,1,0:T(8,128)S(1)}, u32[]{:S(2)}, u32[]{:S(2)}) collective-permute-start(f32[1,8,256]{2,1,0:T(8,128)S(1)} %get-tuple-element.220), channel_id=1, source_target_pairs={{1,0},{2,1},{3,2},{4,3},{5,4},{6,5},{7,6},{8,7},{9,8},{10,9},{11,1... | collective-permute-start | bytes 24584 | tf_op jit(solution)/shard_map/ppermute | solution.py:19
  350.1 5.6 %collective-permute-start.7 = (f32[1,8,256]{2,1,0:T(8,128)S(1)}, f32[1,8,256]{2,1,0:T(8,128)S(1)}, u32[]{:S(2)}, u32[]{:S(2)}) collective-permute-start(f32[1,8,256]{2,1,0:T(8,128)S(1)} %get-tuple-element.221), channel_id=1, source_target_pairs={{0,1},{1,2},{2,3},{3,4},{4,5},{5,6},{6,7},{7,8},{8,9},{9,10},{10,1... | collective-permute-start | bytes 24584 | tf_op jit(solution)/shard_map/ppermute | solution.py:16
  355.8 64.5 %copy-start = (f32[8,8,256]{2,1,0:T(8,128)}, f32[8,8,256]{2,1,0:T(8,128)S(1)}, u32[]{:S(2)}) copy-start(f32[8,8,256]{2,1,0:T(8,128)S(1)} %get-tuple-element.217) | copy-start | bytes 196612
Sparse Core Ops, SparseCore 0:
  10.1 53.0 all-gather.5
where the time goes:
time: 428 us; the launch traced here: 427 us
  other arithmetic  157 us (37%)
  local copies, waits for them, and re-layouts  112 us (26%)
  blocking collectives  86 us (20%)
  waiting for transfers between devices  35.7 us (8%)
  starting transfers between devices  21.8 us (5%)
  between operations  14.3 us (3%)
    reduce_sum x4, other arithmetic, visit(): jnp.sum(warped * warped, axis=0)  83 us
    gather x8, local copies, waits for them, and re-layouts, warp_tile(): lax.dynamic_slice_in_dim(padded, (pad - shift).astype(jnp.int32), tile.sh...  68.4 us
    add x4, other arithmetic, visit(): inner[1] + jnp.sum(warped * warped, axis=0)  64 us
    all_gather x3, blocking collectives, joined(): pieces = jax.tree.map(lambda part: lax.all_gather(part, axis), value)  62.5 us
    all_gather x1, waiting for transfers between devices, per_device(): tiles = lax.all_gather(features, 'view', axis=0, tiled=True)  31.8 us
    all_gather x1, blocking collectives, per_device(): shifts = lax.all_gather(offsets, 'view', axis=0, tiled=True)  23.4 us
    dynamic_slice x8, local copies, waits for them, and re-layouts, per_device(): lax.scan(visit, (blank, blank), (tile_blocks, shift_blocks))  23.2 us
    pad x4, local copies, waits for them, and re-layouts, warp_tile(): padded = jnp.pad(tile, ((0, 0), (0, 0), (pad, 0)))  19.8 us
  transfers between devices with their start and end apart: 9, of which 5 were waited for; matrix products, arithmetic and copies ran while one was open for 0% of the time, Pallas kernels for 0%

commit v1 on v0

v1 whole, which is shorter than its diff:
```python
import functools

import jax
import jax.numpy as jnp
from jax import lax
from jax.experimental import pallas as pl
from jax.experimental.pallas import tpu as pltpu
from jax.sharding import PartitionSpec as P

ITERS = 4
LANES = 128
GROUP = 8


def shifted(x, amount, lane):
    if amount == 0:
        return x
    return jnp.where(lane >= amount, pltpu.roll(x, amount, 1), 0.0)


def kernel(
    n, feat_ref, off_ref, conf_ref, depth_ref, cost_ref, map_ref,
    xs, xr, offv, offs, table, sqs, spad, part, costs, stat_s, stat_r, res,
    local_sem, xs_send, xs_recv, off_send, off_recv, c_send, c_recv, s_send, s_recv, r_send, r_recv,
):
    _, chans, rows, width = feat_ref.shape
    planes = off_ref.shape[-1]
    owned = depth_ref.shape[0]
    groups = n // rows
    cg = chans // groups
    pad = width // 8
    halo = ITERS
    span = 2 * GROUP
    per_window = GROUP // owned
    windows = planes // GROUP
    blocks = windows + 1
    halves = width // LANES
    owners = rows * halves
    me = lax.axis_index("view")
    my_window = me // per_window

    for r in range(rows):
        line = feat_ref[0, :, r, :]
        for g in range(groups):
            xs[r * groups + g] = line[g * cg:(g + 1) * cg]
    offv[me] = off_ref[...]

    barrier = pltpu.get_barrier_semaphore()

    def greet(k, carry):
        pl.semaphore_signal(barrier, inc=1, device_id={"view": lax.rem(me + k, n)})
        return carry

    lax.fori_loop(1, n, greet, 0)
    pl.semaphore_wait(barrier, n - 1)

    def off_copy(slot, peer):
        return pltpu.make_async_remote_copy(
            src_ref=offv.at[slot], dst_ref=offv.at[slot], send_sem=off_send.at[peer],
            recv_sem=off_recv.at[slot], device_id={"view": peer})

    def feat_copy(slot, peer):
        return pltpu.make_async_remote_copy(
            src_ref=xs.at[peer], dst_ref=xr.at[slot], send_sem=xs_send.at[peer],
            recv_sem=xs_recv.at[slot], device_id={"view": peer})

    def send_feat(k, carry):
        peer = lax.rem(me + k, n)
        off_copy(me, peer).start()
        feat_copy(me, peer).start()
        return carry

    lax.fori_loop(1, n, send_feat, 0)

    lane = lax.broadcasted_iota(jnp.int32, (cg, width), 1)

    def build(view, x):
        for o in range(pad):
            table[view * pad + o] = shifted(x, o, lane)
        sqs[pl.ds(view, 1), :] = jnp.sum(x * x, axis=0, keepdims=True)

    build(me, xs[me])

    def receive(k, carry):
        source = lax.rem(me - k + n, n)
        feat_copy(source, source).wait_recv()
        off_copy(source, source).wait_recv()
        build(source, xr[source])
        return carry

    lax.fori_loop(1, n, receive, 0)

    to_scalar = pltpu.make_async_copy(offv, offs, local_sem)
    to_scalar.start()
    chosen = offv[:, 0, :]
    sq = sqs[...]
    lane_n = lax.broadcasted_iota(jnp.int32, (n, width), 1)
    hot = jnp.concatenate(
        [jnp.where(chosen == o, 1.0, 0.0) for o in range(pad)], axis=0)
    sq_all = jnp.concatenate([shifted(sq, o, lane_n) for o in range(pad)], axis=0)
    hot = hot.T.astype(jnp.bfloat16)
    high = sq_all.astype(jnp.bfloat16)
    rest = sq_all - high.astype(jnp.float32)
    mid = rest.astype(jnp.bfloat16)
    low = (rest - mid.astype(jnp.float32)).astype(jnp.bfloat16)
    square = jnp.zeros((planes, width), jnp.float32)
    for piece in (low, mid, high):
        square = square + jnp.dot(hot, piece, preferred_element_type=jnp.float32)
    spad[...] = jnp.zeros_like(spad)
    spad[halo:halo + planes, :] = square * (1.0 / (n * chans))
    to_scalar.wait()

    def cost_copy(slot, peer, window):
        first = pl.multiple_of(window * GROUP, GROUP)
        return pltpu.make_async_remote_copy(
            src_ref=part.at[pl.ds(first, span)], dst_ref=costs.at[slot],
            send_sem=c_send.at[peer], recv_sem=c_recv.at[slot], device_id={"view": peer})

    def block(k, carry):
        j = lax.rem(my_window + 1 + k, blocks)
        sums = []
        for i in range(GROUP):
            p = jnp.clip(j * GROUP + i - halo, 0, planes - 1)
            total = table[offs[0, 0, p]]
            for v in range(1, n):
                total = total + table[v * pad + offs[v, 0, p]]
            sums.append(jnp.sum(total * total, axis=0, keepdims=True))
        first = pl.multiple_of(j * GROUP, GROUP)
        part[pl.ds(first, GROUP), :] = (
            spad[pl.ds(first, GROUP), :]
            - jnp.concatenate(sums, axis=0) * (1.0 / (n * n * chans)))

        @pl.when(jnp.logical_and(k > 0, j > 0))
        def _():
            for m in range(per_window):
                peer = (j - 1) * per_window + m
                cost_copy(me, peer, j - 1).start()

        return carry

    lax.fori_loop(0, blocks, block, 0)
    if per_window > 1:
        for m in range(per_window):
            peer = my_window * per_window + m

            @pl.when(peer != me)
            def _():
                cost_copy(me, peer, my_window).start()

    costs[me] = part[pl.ds(pl.multiple_of(my_window * GROUP, GROUP), span), :]

    def take(k, carry):
        source = lax.rem(me - k + n, n)
        cost_copy(source, source, 0).wait_recv()
        return carry

    lax.fori_loop(1, n, take, 0)

    plane = my_window * GROUP - halo + lax.broadcasted_iota(jnp.int32, (span, width), 0)
    valid = jnp.logical_and(plane >= 0, plane < planes)
    col = lax.broadcasted_iota(jnp.int32, (span, width), 1)
    cost, rate = [], []
    for r in range(rows):
        total = costs[r * groups]
        for g in range(1, groups):
            total = total + costs[r * groups + g]
        cost.append(jnp.where(valid, total, 0.0))
        conf = (conf_ref[r:r + 1, :].astype(jnp.float32) + 1.0) * 0.25
        rate.append(jnp.where(valid, 0.15 * conf, 0.0))
    for step in range(ITERS):
        new = []
        for r in range(rows):
            c = cost[r]
            beside = pltpu.roll(c, 1, 0) + pltpu.roll(c, span - 1, 0)
            if r > 0:
                beside = beside + cost[r - 1]
            if r < rows - 1:
                beside = beside + cost[r + 1]
            beside = beside + jnp.where(col > 0, pltpu.roll(c, 1, 1), 0.0)
            beside = beside + jnp.where(col < width - 1, pltpu.roll(c, width - 1, 1), 0.0)
            new.append(c + rate[r] * (beside - 6.0 * c))
        cost = new

    index = lax.broadcasted_iota(jnp.int32, (owned, width), 0)
    depth = jnp.zeros((owned, width), jnp.float32)
    for i in range(owned):
        depth = jnp.where(index == i, depth_ref[i], depth)
    for r in range(rows):
        own = cost[r][halo:halo + owned]
        for m in range(1, per_window):
            first = halo + m * owned
            own = jnp.where(lax.rem(me, per_window) == m, cost[r][first:first + owned], own)
        cost_ref[:, r, :] = own
        peak = jnp.max(-own, axis=0, keepdims=True)
        weight = jnp.exp(-own - peak)
        soft = jnp.concatenate(
            [peak, jnp.sum(weight, axis=0, keepdims=True),
             jnp.sum(weight * depth, axis=0, keepdims=True)], axis=0)
        for h in range(halves):
            stat_s[r * halves + h] = soft[:, h * LANES:(h + 1) * LANES]

    def stat_copy(slot, peer):
        return pltpu.make_async_remote_copy(
            src_ref=stat_s.at[peer], dst_ref=stat_r.at[slot], send_sem=s_send.at[peer],
            recv_sem=s_recv.at[slot], device_id={"view": peer})

    def res_copy(slot, peer):
        return pltpu.make_async_remote_copy(
            src_ref=res.at[slot], dst_ref=res.at[slot], send_sem=r_send.at[peer],
            recv_sem=r_recv.at[slot], device_id={"view": peer})

    def send_stat(k, carry):
        peer = lax.rem(me + k, n)

        @pl.when(peer < owners)
        def _():
            stat_copy(me, peer).start()

        return carry

    lax.fori_loop(1, n, send_stat, 0)

    @pl.when(me < owners)
    def _():
        stat_r[me] = stat_s[me]

        def wait_stat(k, carry):
            source = lax.rem(me - k + n, n)
            stat_copy(source, me).wait_recv()
            return carry

        lax.fori_loop(1, n, wait_stat, 0)
        got = stat_r[...]
        top = jnp.max(got[:, 0, :], axis=0, keepdims=True)
        scale = jnp.exp(got[:, 0, :] - top)
        denom = jnp.sum(got[:, 1, :] * scale, axis=0, keepdims=True)
        numer = jnp.sum(got[:, 2, :] * scale, axis=0, keepdims=True)
        res[me] = numer / denom

        def send_res(k, carry):
            res_copy(me, lax.rem(me + k, n)).start()
            return carry

        lax.fori_loop(1, n, send_res, 0)

    def finish(k, carry):
        peer = lax.rem(me + k, n)
        feat_copy(me, peer).wait_send()
        off_copy(me, peer).wait_send()
        cost_copy(me, peer, 0).wait_send()

        @pl.when(peer < owners)
        def _():
            stat_copy(me, peer).wait_send()
            res_copy(peer, peer).wait_recv()

        @pl.when(me < owners)
        def _():
            res_copy(me, peer).wait_send()

        return carry

    lax.fori_loop(1, n, finish, 0)
    for r in range(rows):
        for h in range(halves):
            map_ref[r:r + 1, h * LANES:(h + 1) * LANES] = res[r * halves + h]


def per_device(features, offsets, conf_bins, plane_depths):
    n = lax.axis_size("view")
    _, chans, rows, width = features.shape
    planes = offsets.shape[-1]
    owned = plane_depths.shape[0]
    cg = chans * rows // n
    pad = width // 8
    owners = rows * width // LANES
    padded = planes + 2 * ITERS
    f32 = jnp.float32
    vmem = pl.BlockSpec(memory_space=pltpu.VMEM)
    dma = pltpu.SemaphoreType.DMA
    return pl.pallas_call(
        functools.partial(kernel, n),
        out_shape=(
            jax.ShapeDtypeStruct((owned, rows, width), f32),
            jax.ShapeDtypeStruct((rows, width), f32),
        ),
        in_specs=[vmem, vmem, vmem, pl.BlockSpec(memory_space=pltpu.SMEM)],
        out_specs=(vmem, vmem),
        scratch_shapes=[
            pltpu.VMEM((n, cg, width), f32),
            pltpu.VMEM((n, cg, width), f32),
            pltpu.VMEM((n, 1, planes), jnp.int32),
            pltpu.SMEM((n, 1, planes), jnp.int32),
            pltpu.VMEM((n * pad, cg, width), f32),
            pltpu.VMEM((n, width), f32),
            pltpu.VMEM((padded, width), f32),
            pltpu.VMEM((padded, width), f32),
            pltpu.VMEM((n, 2 * GROUP, width), f32),
            pltpu.VMEM((owners, 3, LANES), f32),
            pltpu.VMEM((n, 3, LANES), f32),
            pltpu.VMEM((owners, 1, LANES), f32),
            dma,
        ] + [dma((n,)) for _ in range(10)],
        compiler_params=pltpu.CompilerParams(collective_id=0, has_side_effects=True,
                                             vmem_limit_bytes=60 << 20),
    )(features, offsets, conf_bins, plane_depths)


def solution(mesh):
    in_specs = (
        P(("grp", "view"), None, None, None),
        P(("grp", "view"), None),
        P("grp", None),
        P("view"),
    )
    out_specs = (P("view", "grp", None), P("grp", None))
    return jax.shard_map(
        per_device, mesh=mesh, in_specs=in_specs, out_specs=out_specs, check_vma=False
    )
```

time: 428 us -> 38.4 us (0.09)
  other arithmetic: 157 us -> 0 us
  local copies, waits for them, and re-layouts: 112 us -> 2.08 us
  blocking collectives: 86 us -> 0 us
  waiting for transfers between devices: 35.7 us -> 0 us
  Pallas kernels: 0 us -> 35.5 us
  starting transfers between devices: 21.8 us -> 0 us
  between operations: 14.3 us -> 0.65 us
    reduce_sum x6 -> x0, other arithmetic: 91.2 us -> none  [the longest x4 83 us: visit(): jnp.sum(warped * warped, axis=0)]
    all_gather x4 -> x0, blocking collectives: 86 us -> none  [the longest x3 62.5 us: joined(): pieces = jax.tree.map(lambda part: lax.all_gather(part, axis), value)]
    gather x8 -> x0, local copies, waits for them, and re-layouts: 68.4 us -> none  [warp_tile(): lax.dynamic_slice_in_dim(padded, (pad - shift).astype(jnp.int32), tile.sh...]
    add x37 -> x0, other arithmetic: 64.9 us -> none  [the longest x4 64 us: visit(): inner[1] + jnp.sum(warped * warped, axis=0)]
    pallas_call x0 -> x1, Pallas kernels: none -> 35.5 us  [per_device(): pl.pallas_call(functools.partial(kernel, n), out_shape=(jax.ShapeDtypeStr...]
    all_gather x1 -> x0, waiting for transfers between devices: 31.8 us -> none  [per_device(): tiles = lax.all_gather(features, 'view', axis=0, tiled=True)]
    dynamic_slice x9 -> x0, local copies, waits for them, and re-layouts: 23.3 us -> none  [the longest x8 23.2 us: per_device(): lax.scan(visit, (blank, blank), (tile_blocks, shift_blocks))]
    ppermute x8 -> x0, starting transfers between devices: 21.7 us -> none  [the longest x4 16.6 us: extended(): lax.ppermute(lax.slice_in_dim(block, block.shape[dim] - width, None, axis...]
  transfers between devices with their start and end apart: 9 -> 0, of which waited for: 5 -> 0; matrix products, arithmetic and copies ran while one was open for 0% -> 0% of each run, Pallas kernels for 0% -> 0%
where the time goes in v1:
time: 38.4 us; the launch traced here: 38.2 us
  Pallas kernels  35.5 us (92%)
  local copies, waits for them, and re-layouts  2.08 us (5%)
  between operations  0.65 us (2%)
    pallas_call x1, Pallas kernels, per_device(): pl.pallas_call(functools.partial(kernel, n), out_shape=(jax.ShapeDtypeStr...  35.5 us
    unnamed x4, local copies, waits for them, and re-layouts  2.08 us

profile of v1, /device:TPU:0, one launch (start us, length us, event | category | flops | bytes accessed | tf_op | source)
XLA Modules:
  0.0 38.2 jit_solution(5153337689523539014)
XLA Ops:
  0.6 35.5 %shard_map.59 = (f32[8,8,256]{2,1,0:T(8,128)}, f32[8,256]{1,0:T(8,128)}) custom-call(f32[1,32,8,256]{3,2,1,0:T(8,128)} %feat_ref.1, s32[1,128]{1,0:T(1,128)} %off_ref.1, s32[8,256]{1,0:T(8,128)} %conf_ref.1, f32[8]{0:T(128)} %depth_ref.1), custom_call_target="tpu_custom_call" | custom-call | tf_op jit(solution)/shard_map/pallas_call | solution.py:281
  36.2 0.0 copy-start
  36.2 1.5 %copy.8 = f32[8,8,256]{2,1,0:T(8,128)} copy(f32[8,8,256]{2,1,0:T(8,128)} %get-tuple-element.4) | data formatting | bytes 131072
  37.6 0.0 copy-done
  37.6 0.6 %copy.9 = f32[8,256]{1,0:T(8,128)} copy(f32[8,256]{1,0:T(8,128)S(1)} %copy-done) | data formatting | bytes 16384
Async XLA Ops:
  36.2 1.5 %copy-start = (f32[8,256]{1,0:T(8,128)S(1)}, f32[8,256]{1,0:T(8,128)}, u32[]{:S(2)}) copy-start(f32[8,256]{1,0:T(8,128)} %get-tuple-element.5) | copy-start | bytes 24580

commit v2 on v1

--- a/solution.py
+++ b/solution.py
@@ -20,7 +20,7 @@
 
 def kernel(
     n, feat_ref, off_ref, conf_ref, depth_ref, cost_ref, map_ref,
-    xs, xr, offv, offs, table, sqs, spad, part, costs, stat_s, stat_r, res,
+    feat, xs, xr, offv, offs, table, sqs, spad, part, costs, stat_s, stat_r, res,
     local_sem, xs_send, xs_recv, off_send, off_recv, c_send, c_recv, s_send, s_recv, r_send, r_recv,
 ):
     _, chans, rows, width = feat_ref.shape
@@ -34,24 +34,29 @@
     per_window = GROUP // owned
     windows = planes // GROUP
     blocks = windows + 1
-    halves = width // LANES
-    owners = rows * halves
+    owners, _, share = stat_s.shape
+    parts = width // share
+    first_owner = (n - owners) // 2
     me = lax.axis_index("view")
     my_window = me // per_window
-
+    near = max(1, 4 // per_window)
+    last_window = my_window // near * near + near - 1
+
+    barrier = pltpu.get_barrier_semaphore()
+
+    def greet(k, carry):
+        pl.semaphore_signal(barrier, inc=1, device_id={"view": lax.rem(me + k, n)})
+        return carry
+
+    lax.fori_loop(1, n, greet, 0)
+    fetch = pltpu.make_async_copy(feat_ref.at[0], feat, local_sem)
+    fetch.start()
+    offv[me] = off_ref[...]
+    fetch.wait()
     for r in range(rows):
-        line = feat_ref[0, :, r, :]
+        line = feat[:, r, :]
         for g in range(groups):
             xs[r * groups + g] = line[g * cg:(g + 1) * cg]
-    offv[me] = off_ref[...]
-
-    barrier = pltpu.get_barrier_semaphore()
-
-    def greet(k, carry):
-        pl.semaphore_signal(barrier, inc=1, device_id={"view": lax.rem(me + k, n)})
-        return carry
-
-    lax.fori_loop(1, n, greet, 0)
     pl.semaphore_wait(barrier, n - 1)
 
     def off_copy(slot, peer):
@@ -116,8 +121,16 @@
             src_ref=part.at[pl.ds(first, span)], dst_ref=costs.at[slot],
             send_sem=c_send.at[peer], recv_sem=c_recv.at[slot], device_id={"view": peer})
 
+    def send_cost(window):
+        for m in range(per_window):
+            peer = window * per_window + m
+
+            @pl.when(peer != me)
+            def _():
+                cost_copy(me, peer, window).start()
+
     def block(k, carry):
-        j = lax.rem(my_window + 1 + k, blocks)
+        j = lax.rem(last_window + 1 + k, blocks)
         sums = []
         for i in range(GROUP):
             p = jnp.clip(j * GROUP + i - halo, 0, planes - 1)
@@ -132,21 +145,12 @@
 
         @pl.when(jnp.logical_and(k > 0, j > 0))
         def _():
-            for m in range(per_window):
-                peer = (j - 1) * per_window + m
-                cost_copy(me, peer, j - 1).start()
+            send_cost(j - 1)
 
         return carry
 
     lax.fori_loop(0, blocks, block, 0)
-    if per_window > 1:
-        for m in range(per_window):
-            peer = my_window * per_window + m
-
-            @pl.when(peer != me)
-            def _():
-                cost_copy(me, peer, my_window).start()
-
+    send_cost(last_window)
     costs[me] = part[pl.ds(pl.multiple_of(my_window * GROUP, GROUP), span), :]
 
     def take(k, carry):
@@ -196,37 +200,39 @@
         soft = jnp.concatenate(
             [peak, jnp.sum(weight, axis=0, keepdims=True),
              jnp.sum(weight * depth, axis=0, keepdims=True)], axis=0)
-        for h in range(halves):
-            stat_s[r * halves + h] = soft[:, h * LANES:(h + 1) * LANES]
-
-    def stat_copy(slot, peer):
-        return pltpu.make_async_remote_copy(
-            src_ref=stat_s.at[peer], dst_ref=stat_r.at[slot], send_sem=s_send.at[peer],
-            recv_sem=s_recv.at[slot], device_id={"view": peer})
-
-    def res_copy(slot, peer):
-        return pltpu.make_async_remote_copy(
-            src_ref=res.at[slot], dst_ref=res.at[slot], send_sem=r_send.at[peer],
-            recv_sem=r_recv.at[slot], device_id={"view": peer})
+        for h in range(parts):
+            stat_s[r * parts + h] = soft[:, h * share:(h + 1) * share]
+
+    mine = me - first_owner
+    is_owner = jnp.logical_and(mine >= 0, mine < owners)
+
+    def stat_copy(slot, owner):
+        return pltpu.make_async_remote_copy(
+            src_ref=stat_s.at[owner], dst_ref=stat_r.at[slot], send_sem=s_send.at[owner],
+            recv_sem=s_recv.at[slot], device_id={"view": owner + first_owner})
+
+    def res_copy(owner, peer):
+        return pltpu.make_async_remote_copy(
+            src_ref=res.at[owner], dst_ref=res.at[owner], send_sem=r_send.at[peer],
+            recv_sem=r_recv.at[owner], device_id={"view": peer})
 
     def send_stat(k, carry):
-        peer = lax.rem(me + k, n)
-
-        @pl.when(peer < owners)
+        owner = lax.rem(me + k, owners)
+
+        @pl.when(owner != mine)
         def _():
-            stat_copy(me, peer).start()
-
-        return carry
-
-    lax.fori_loop(1, n, send_stat, 0)
-
-    @pl.when(me < owners)
+            stat_copy(me, owner).start()
+
+        return carry
+
+    lax.fori_loop(0, owners, send_stat, 0)
+
+    @pl.when(is_owner)
     def _():
-        stat_r[me] = stat_s[me]
+        stat_r[me] = stat_s[mine]
 
         def wait_stat(k, carry):
-            source = lax.rem(me - k + n, n)
-            stat_copy(source, me).wait_recv()
+            stat_copy(lax.rem(me - k + n, n), mine).wait_recv()
             return carry
 
         lax.fori_loop(1, n, wait_stat, 0)
@@ -235,10 +241,10 @@
         scale = jnp.exp(got[:, 0, :] - top)
         denom = jnp.sum(got[:, 1, :] * scale, axis=0, keepdims=True)
         numer = jnp.sum(got[:, 2, :] * scale, axis=0, keepdims=True)
-        res[me] = numer / denom
+        res[mine] = numer / denom
 
         def send_res(k, carry):
-            res_copy(me, lax.rem(me + k, n)).start()
+            res_copy(mine, lax.rem(me + k, n)).start()
             return carry
 
         lax.fori_loop(1, n, send_res, 0)
@@ -249,21 +255,26 @@
         off_copy(me, peer).wait_send()
         cost_copy(me, peer, 0).wait_send()
 
-        @pl.when(peer < owners)
+        @pl.when(is_owner)
         def _():
-            stat_copy(me, peer).wait_send()
-            res_copy(peer, peer).wait_recv()
-
-        @pl.when(me < owners)
+            res_copy(mine, peer).wait_send()
+
+        return carry
+
+    lax.fori_loop(1, n, finish, 0)
+
+    def collect(owner, carry):
+        @pl.when(owner != mine)
         def _():
-            res_copy(me, peer).wait_send()
-
-        return carry
-
-    lax.fori_loop(1, n, finish, 0)
+            stat_copy(me, owner).wait_send()
+            res_copy(owner, owner + first_owner).wait_recv()
+
+        return carry
+
+    lax.fori_loop(0, owners, collect, 0)
     for r in range(rows):
-        for h in range(halves):
-            map_ref[r:r + 1, h * LANES:(h + 1) * LANES] = res[r * halves + h]
+        for h in range(parts):
+            map_ref[r:r + 1, h * share:(h + 1) * share] = res[r * parts + h]
 
 
 def per_device(features, offsets, conf_bins, plane_depths):
@@ -273,7 +284,9 @@
     owned = plane_depths.shape[0]
     cg = chans * rows // n
     pad = width // 8
-    owners = rows * width // LANES
+    chunks = rows * width // LANES
+    share = min(max(1, chunks // max(1, n // 2)) * LANES, width)
+    owners = rows * width // share
     padded = planes + 2 * ITERS
     f32 = jnp.float32
     vmem = pl.BlockSpec(memory_space=pltpu.VMEM)
@@ -284,9 +297,10 @@
             jax.ShapeDtypeStruct((owned, rows, width), f32),
             jax.ShapeDtypeStruct((rows, width), f32),
         ),
-        in_specs=[vmem, vmem, vmem, pl.BlockSpec(memory_space=pltpu.SMEM)],
+        in_specs=[pl.BlockSpec(memory_space=pl.ANY), vmem, vmem, pl.BlockSpec(memory_space=pltpu.SMEM)],
         out_specs=(vmem, vmem),
         scratch_shapes=[
+            pltpu.VMEM((chans, rows, width), f32),
             pltpu.VMEM((n, cg, width), f32),
             pltpu.VMEM((n, cg, width), f32),
             pltpu.VMEM((n, 1, planes), jnp.int32),
@@ -296,9 +310,9 @@
             pltpu.VMEM((padded, width), f32),
             pltpu.VMEM((padded, width), f32),
             pltpu.VMEM((n, 2 * GROUP, width), f32),
-            pltpu.VMEM((owners, 3, LANES), f32),
-            pltpu.VMEM((n, 3, LANES), f32),
-            pltpu.VMEM((owners, 1, LANES), f32),
+            pltpu.VMEM((owners, 3, share), f32),
+            pltpu.VMEM((n, 3, share), f32),
+            pltpu.VMEM((owners, 1, share), f32),
             dma,
         ] + [dma((n,)) for _ in range(10)],
         compiler_params=pltpu.CompilerParams(collective_id=0, has_side_effects=True,

time: 38.4 us -> 37 us (0.964)
  Pallas kernels: 35.5 us -> 34 us
    pallas_call x1, Pallas kernels: 35.5 us -> 34 us  [per_device(): pl.pallas_call(functools.partial(kernel, n), out_shape=(jax.ShapeDtypeStr...]
where the time goes in v2:
time: 37 us; the launch traced here: 36.7 us
  Pallas kernels  34 us (92%)
  local copies, waits for them, and re-layouts  2.08 us (6%)
  between operations  0.65 us (2%)
    pallas_call x1, Pallas kernels, per_device(): pl.pallas_call(functools.partial(kernel, n), out_shape=(jax.ShapeDtypeStr...  34 us
    unnamed x4, local copies, waits for them, and re-layouts  2.08 us

profile of v2, /device:TPU:0, one launch (start us, length us, event | category | flops | bytes accessed | tf_op | source)
XLA Modules:
  0.0 36.7 jit_solution(10634666518403972356)
XLA Ops:
  0.6 34.0 %shard_map.59 = (f32[8,8,256]{2,1,0:T(8,128)}, f32[8,256]{1,0:T(8,128)}) custom-call(f32[1,32,8,256]{3,2,1,0:T(8,128)} %feat_ref.1, s32[1,128]{1,0:T(1,128)} %off_ref.1, s32[8,256]{1,0:T(8,128)} %conf_ref.1, f32[8]{0:T(128)} %depth_ref.1), custom_call_target="tpu_custom_call" | custom-call | tf_op jit(solution)/shard_map/pallas_call | solution.py:294
  34.6 0.0 copy-start
  34.7 1.5 %copy.8 = f32[8,8,256]{2,1,0:T(8,128)} copy(f32[8,8,256]{2,1,0:T(8,128)} %get-tuple-element.4) | data formatting | bytes 131072
  36.1 0.0 copy-done
  36.1 0.6 %copy.9 = f32[8,256]{1,0:T(8,128)} copy(f32[8,256]{1,0:T(8,128)S(1)} %copy-done) | data formatting | bytes 16384
Async XLA Ops:
  34.6 1.5 %copy-start = (f32[8,256]{1,0:T(8,128)S(1)}, f32[8,256]{1,0:T(8,128)}, u32[]{:S(2)}) copy-start(f32[8,256]{1,0:T(8,128)} %get-tuple-element.5) | copy-start | bytes 24580

commit v3 on v2

--- a/solution.py
+++ b/solution.py
@@ -277,6 +277,11 @@
             map_ref[r:r + 1, h * share:(h + 1) * share] = res[r * parts + h]
 
 
+def hand_on(cost_in, map_in, cost_out, map_out):
+    cost_out[...] = cost_in[...]
+    map_out[...] = map_in[...]
+
+
 def per_device(features, offsets, conf_bins, plane_depths):
     n = lax.axis_size("view")
     _, chans, rows, width = features.shape
@@ -291,7 +296,7 @@
     f32 = jnp.float32
     vmem = pl.BlockSpec(memory_space=pltpu.VMEM)
     dma = pltpu.SemaphoreType.DMA
-    return pl.pallas_call(
+    outputs = pl.pallas_call(
         functools.partial(kernel, n),
         out_shape=(
             jax.ShapeDtypeStruct((owned, rows, width), f32),
@@ -318,6 +323,12 @@
         compiler_params=pltpu.CompilerParams(collective_id=0, has_side_effects=True,
                                              vmem_limit_bytes=60 << 20),
     )(features, offsets, conf_bins, plane_depths)
+    return pl.pallas_call(
+        hand_on,
+        out_shape=tuple(jax.ShapeDtypeStruct(x.shape, x.dtype) for x in outputs),
+        in_specs=[vmem, vmem],
+        out_specs=(vmem, vmem),
+    )(*outputs)
 
 
 def solution(mesh):

time: 37 us -> 36.4 us (0.984)
  local copies, waits for them, and re-layouts: 2.08 us -> 0 us
  Pallas kernels: 34 us -> 35.5 us
    unnamed x4 -> x0, local copies, waits for them, and re-layouts: 2.08 us -> none
    pallas_call x0 -> x1, Pallas kernels: none -> 1.48 us  [per_device(): pl.pallas_call(hand_on, out_shape=tuple((jax.ShapeDtypeStruct(x.shape, x....]
where the time goes in v3:
time: 36.4 us; the launch traced here: 36.1 us
  Pallas kernels  35.5 us (98%)
  between operations  0.64 us (2%)
    pallas_call x1, Pallas kernels, per_device(): pl.pallas_call(functools.partial(kernel, n), out_shape=(jax.ShapeDtypeStr...  34 us
    pallas_call x1, Pallas kernels, per_device(): pl.pallas_call(hand_on, out_shape=tuple((jax.ShapeDtypeStruct(x.shape, x....  1.48 us

profile of v3, /device:TPU:0, one launch (start us, length us, event | category | flops | bytes accessed | tf_op | source)
XLA Modules:
  0.0 36.1 jit_solution(15703117118849899863)
XLA Ops:
  0.6 34.0 %shard_map.59 = (f32[8,8,256]{2,1,0:T(8,128)}, f32[8,256]{1,0:T(8,128)}) custom-call(f32[1,32,8,256]{3,2,1,0:T(8,128)} %feat_ref.1, s32[1,128]{1,0:T(1,128)} %off_ref.1, s32[8,256]{1,0:T(8,128)} %conf_ref.1, f32[8]{0:T(128)} %depth_ref.1), custom_call_target="tpu_custom_call" | custom-call | tf_op jit(solution)/shard_map/pallas_call | solution.py:299
  34.6 1.5 %shard_map.60 = (f32[8,8,256]{2,1,0:T(8,128)}, f32[8,256]{1,0:T(8,128)}) custom-call(f32[8,8,256]{2,1,0:T(8,128)} %get-tuple-element.4.cost_in, f32[8,256]{1,0:T(8,128)} %get-tuple-element.5.map_in), custom_call_target="tpu_custom_call" | custom-call | tf_op jit(solution)/shard_map/pallas_call | solution.py:326
